TPU v7x, 32 devices: a whole 2x2x4 slice. The times are simulated.
32 devices in a mesh: side: 4 (over y, core), batch: 8 (over z, x).
Axes of the slice: x: 2, y: 2, z: 4, core: 2. Of those that a mesh axis runs over, the one named last changes fastest.
Arguments:
- hidden_in: bfloat16 [4, 8, 1024, 512], P('side', 'batch'), may hold values from -6 to 6
- segments: int32 [4, 8, 1024], P('side', 'batch'), may hold values from -1 to 31, as said below
- query_cls: int32 [8, 32], P('batch'), may hold values from 0 to 930, as said below
- passage_cls: int32 [4, 8, 5], P('side', 'batch'), may hold values from 0 to 800, as said below
- pair_passage: int32 [256], P('batch'), may hold values from 0 to 119
- passage_cluster: int32 [120], replicated, may hold values from 0 to 31
- teacher: float32 [256, 120], P('batch'), may hold values from -6 to 6
- query_weight: bfloat16 [512, 512], replicated, may hold values from -0.25 to 0.25
- query_bias: float32 [512], replicated, may hold values from -3 to 3
- key_weight: bfloat16 [512, 512], replicated, may hold values from -0.25 to 0.25
- value_weight: bfloat16 [512, 512], replicated, may hold values from -0.25 to 0.25
- value_bias: float32 [512], replicated, may hold values from -1.75 to 1.75
- out_weight: bfloat16 [512, 512], replicated, may hold values from -1 to 1
- out_bias: float32 [512], replicated, may hold values from -1.75 to 1.75
- first_gain: float32 [512], replicated, may hold values from 0.5 to 1.5
- first_shift: float32 [512], replicated, may hold values from -1.75 to 1.75
- inner_weight: bfloat16 [512, 2048], replicated, may hold values from -0.25 to 0.25
- inner_bias: float32 [2048], replicated, may hold values from -3 to 3
- outer_weight: bfloat16 [2048, 512], replicated, may hold values from -0.125 to 0.125
- outer_bias: float32 [512], replicated, may hold values from -1.75 to 1.75
- second_gain: float32 [512], replicated, may hold values from 0.5 to 1.5
- second_shift: float32 [512], replicated, may hold values from -1.75 to 1.75
Outputs:
- loss: float32 [], replicated
- rows_out: bfloat16 [4, 8, 1024, 512], P('side', 'batch')
- input_grad: bfloat16 [4, 8, 1024, 512], P('side', 'batch')
- grad_query_weight: float32 [512, 512], replicated
- grad_query_bias: float32 [512], replicated
- grad_key_weight: float32 [512, 512], replicated
- grad_value_weight: float32 [512, 512], replicated
- grad_value_bias: float32 [512], replicated
- grad_out_weight: float32 [512, 512], replicated
- grad_out_bias: float32 [512], replicated
- grad_first_gain: float32 [512], replicated
- grad_first_shift: float32 [512], replicated
- grad_inner_weight: float32 [512, 2048], replicated
- grad_inner_bias: float32 [2048], replicated
- grad_outer_weight: float32 [2048, 512], replicated
- grad_outer_bias: float32 [512], replicated
- grad_second_gain: float32 [512], replicated
- grad_second_shift: float32 [512], replicated
Inputs may be any that keep to these rules, and one draw needn't show every extreme that they name: `segments`: in every row segment numbers start at 0 and never fall; the tokens after the last segment carry -1. A row of the first group holds 32 queries of 8 to 30 tokens, one of exactly 30; a row of another group holds 5 passages of 50 to 200 tokens, one of exactly 200. `query_cls`: the first token of each segment of the first group's row, in order. `passage_cls`: the first token of each passage of the row, in order; in the first group it holds the first 5 query starts, which nothing uses.
All inputs are finite; a program needn't handle non-finite values.
Results may differ from a plain program's by a relative error of at most 0.02.
Values may be sent and summed in bfloat16 or wider, within the bound.
No kernel may reach another device: no remote copies, remote signals or barrier semaphores. Data moves between devices by JAX's collectives and lax.ppermute only.
A program may use at most 192 MiB of HBM per device.

v0:
```python
from functools import partial
import jax
import jax.numpy as jnp
from jax import lax
from jax.sharding import PartitionSpec as P

HEADS = 8
HD = 64
EPSILON = 1e-05
NEG_FILL = -1e30


def norm_forward(summed, gain, shift):
    centre = jnp.mean(summed, axis=1, keepdims=True)
    deviation = summed - centre
    inverse = lax.rsqrt(jnp.mean(deviation * deviation, axis=1, keepdims=True) + EPSILON)
    normed = deviation * inverse
    return (normed * gain + shift, normed, inverse)


def norm_backward(upstream, normed, inverse, gain):
    scaled_up = upstream * gain
    inner_mean = jnp.mean(scaled_up, axis=1, keepdims=True)
    cross_mean = jnp.mean(scaled_up * normed, axis=1, keepdims=True)
    grad_in = inverse * (scaled_up - inner_mean - normed * cross_mean)
    return (grad_in, jnp.sum(upstream * normed, axis=0), jnp.sum(upstream, axis=0))


def contract_rows(left, right):
    return lax.dot_general(
        left, right, (((0,), (0,)), ((), ())), preferred_element_type=jnp.float32
    )


def times_transposed(left, right):
    return lax.dot_general(
        left, right, (((1,), (1,)), ((), ())), preferred_element_type=jnp.float32
    )


def block_scores(query_part, keys3, seg_part, seg_all, score_scale):
    raw = (
        jnp.einsum("qhd,khd->hqk", query_part, keys3, preferred_element_type=jnp.float32)
        * score_scale
    )
    same = seg_part[:, None] == seg_all[None, :]
    return jnp.where(same[None], raw, NEG_FILL)


def body(
    hidden_in,
    segments,
    query_cls,
    passage_cls,
    pair_passage,
    passage_cluster,
    teacher,
    query_weight,
    query_bias,
    key_weight,
    value_weight,
    value_bias,
    out_weight,
    out_bias,
    first_gain,
    first_shift,
    inner_weight,
    inner_bias,
    outer_weight,
    outer_bias,
    second_gain,
    second_shift,
):
    count_tok = hidden_in.shape[2]
    model_width = hidden_in.shape[3]
    tokens = hidden_in.reshape(count_tok, model_width)
    seg_ids = segments.reshape(count_tok)
    query_idx = query_cls.reshape(-1)
    passage_idx = passage_cls.reshape(-1)
    is_query = lax.axis_index("side") == 0
    score_scale = HD ** (-0.5)
    cls_scale = model_width ** (-0.5)
    block_rows = min(512, count_tok)
    queries = (
        jnp.dot(tokens, query_weight, preferred_element_type=jnp.float32) + query_bias
    ).astype(jnp.bfloat16)
    keys_low = jnp.dot(tokens, key_weight, preferred_element_type=jnp.float32).astype(jnp.bfloat16)
    values_low = (
        jnp.dot(tokens, value_weight, preferred_element_type=jnp.float32) + value_bias
    ).astype(jnp.bfloat16)
    queries3 = queries.reshape(count_tok, HEADS, HD)
    keys3 = keys_low.reshape(count_tok, HEADS, HD)
    values3 = values_low.reshape(count_tok, HEADS, HD)
    contexts = []
    log_parts = []
    for first_row in range(0, count_tok, block_rows):
        scores = block_scores(
            queries3[first_row : first_row + block_rows],
            keys3,
            seg_ids[first_row : first_row + block_rows],
            seg_ids,
            score_scale,
        )
        peak = jnp.max(scores, axis=2, keepdims=True)
        expo = jnp.exp(scores - peak)
        total = jnp.sum(expo, axis=2, keepdims=True)
        probs_low = (expo / total).astype(jnp.bfloat16)
        contexts.append(
            jnp.einsum("hqk,khd->qhd", probs_low, values3, preferred_element_type=jnp.float32)
        )
        log_parts.append(peak + jnp.log(total))
    context_low = (
        jnp.concatenate(contexts, axis=0).reshape(count_tok, model_width).astype(jnp.bfloat16)
    )
    log_totals = jnp.concatenate(log_parts, axis=1)
    attended = tokens.astype(jnp.float32) + (
        jnp.dot(context_low, out_weight, preferred_element_type=jnp.float32) + out_bias
    )
    first, first_hat, first_inv = norm_forward(attended, first_gain, first_shift)
    first_low = first.astype(jnp.bfloat16)
    pre = jnp.dot(first_low, inner_weight, preferred_element_type=jnp.float32) + inner_bias
    gelu_exact = partial(jax.nn.gelu, approximate=False)
    activated, gelu_pull = jax.vjp(gelu_exact, pre)
    active_low = activated.astype(jnp.bfloat16)
    second = first + (
        jnp.dot(active_low, outer_weight, preferred_element_type=jnp.float32) + outer_bias
    )
    final, second_hat, second_inv = norm_forward(second, second_gain, second_shift)
    final_low = final.astype(jnp.bfloat16)
    query_vectors = final_low[query_idx]
    passage_vectors = final_low[passage_idx]
    gathered = lax.all_gather(passage_vectors, ("side", "batch"), axis=0, tiled=True)
    pass_count = teacher.shape[1]
    front = gathered.shape[0] - pass_count
    passages_all = gathered[front:]
    scores_cls = times_transposed(query_vectors, passages_all) * cls_scale
    columns = jnp.arange(pass_count, dtype=jnp.int32)
    is_pair = pair_passage[:, None] == columns[None, :]
    query_cluster = jnp.sum(jnp.where(is_pair, passage_cluster[None, :], 0), axis=1)
    counted = (
        (passage_cluster[None, :] == query_cluster[:, None]) & jnp.logical_not(is_pair) & is_query
    )
    pair_score = jnp.sum(jnp.where(is_pair, scores_cls, 0.0), axis=1, keepdims=True)
    resid = jnp.where(counted, pair_score - scores_cls - teacher, 0.0)
    loss_sq = jnp.sum(resid * resid)
    loss_count = jnp.sum(counted.astype(jnp.float32))
    grad_score = jnp.where(is_pair, jnp.sum(resid, axis=1, keepdims=True), 0.0) - resid
    grad_score_low = (grad_score * cls_scale).astype(jnp.bfloat16)
    grad_queries = jnp.dot(grad_score_low, passages_all, preferred_element_type=jnp.float32)
    padded = jnp.concatenate(
        [jnp.zeros((front, grad_score_low.shape[0]), jnp.bfloat16), grad_score_low.T], axis=0
    )
    grad_passages = lax.psum_scatter(
        jnp.dot(
            lax.slice_in_dim(
                padded, 0, passage_vectors.shape[0] * lax.axis_size(("side", "batch")), axis=0
            ),
            query_vectors,
            preferred_element_type=jnp.float32,
        ),
        ("side", "batch"),
        scatter_dimension=0,
        tiled=True,
    )
    zero_rows = jnp.zeros((count_tok, model_width), jnp.float32)
    grad_final = jnp.where(
        is_query,
        zero_rows.at[query_idx].add(grad_queries),
        zero_rows.at[passage_idx].add(grad_passages),
    )
    grad_second, grad_second_gain, grad_second_shift = norm_backward(
        grad_final, second_hat, second_inv, second_gain
    )
    grad_outer_bias = jnp.sum(grad_second, axis=0)
    second_low = grad_second.astype(jnp.bfloat16)
    grad_outer_weight = contract_rows(active_low, second_low)
    grad_active = times_transposed(second_low, outer_weight)
    grad_pre = gelu_pull(grad_active)[0]
    grad_inner_bias = jnp.sum(grad_pre, axis=0)
    pre_low = grad_pre.astype(jnp.bfloat16)
    grad_inner_weight = contract_rows(first_low, pre_low)
    grad_first = times_transposed(pre_low, inner_weight) + grad_second
    ffn_parts = (
        grad_inner_weight,
        grad_inner_bias,
        grad_outer_weight,
        grad_outer_bias,
        grad_second_gain,
        grad_second_shift,
    )
    grad_attended, grad_first_gain, grad_first_shift = norm_backward(
        grad_first, first_hat, first_inv, first_gain
    )
    grad_out_bias = jnp.sum(grad_attended, axis=0)
    attended_low = grad_attended.astype(jnp.bfloat16)
    grad_out_weight = contract_rows(context_low, attended_low)
    grad_context = times_transposed(attended_low, out_weight).astype(jnp.bfloat16)
    grad_context3 = grad_context.reshape(count_tok, HEADS, HD)
    grad_query_parts = []
    grad_keys = jnp.zeros((count_tok, HEADS, HD), jnp.float32)
    grad_values = jnp.zeros((count_tok, HEADS, HD), jnp.float32)
    for first_row in range(0, count_tok, block_rows):
        query_part = queries3[first_row : first_row + block_rows]
        scores = block_scores(
            query_part, keys3, seg_ids[first_row : first_row + block_rows], seg_ids, score_scale
        )
        probs = jnp.exp(scores - log_totals[:, first_row : first_row + block_rows])
        upstream = grad_context3[first_row : first_row + block_rows]
        grad_probs = jnp.einsum(
            "qhd,khd->hqk", upstream, values3, preferred_element_type=jnp.float32
        )
        row_dot = jnp.sum(probs * grad_probs, axis=2, keepdims=True)
        grad_scores = (probs * (grad_probs - row_dot)).astype(jnp.bfloat16)
        grad_query_parts.append(
            jnp.einsum("hqk,khd->qhd", grad_scores, keys3, preferred_element_type=jnp.float32)
            * score_scale
        )
        grad_keys = (
            grad_keys
            + jnp.einsum(
                "hqk,qhd->khd", grad_scores, query_part, preferred_element_type=jnp.float32
            )
            * score_scale
        )
        grad_values = grad_values + jnp.einsum(
            "hqk,qhd->khd", probs.astype(jnp.bfloat16), upstream, preferred_element_type=jnp.float32
        )
    grad_query = jnp.concatenate(grad_query_parts, axis=0).reshape(count_tok, model_width)
    grad_keys = grad_keys.reshape(count_tok, model_width)
    grad_values = grad_values.reshape(count_tok, model_width)
    grad_query_bias = jnp.sum(grad_query, axis=0)
    grad_value_bias = jnp.sum(grad_values, axis=0)
    query_low = grad_query.astype(jnp.bfloat16)
    key_low = grad_keys.astype(jnp.bfloat16)
    value_low = grad_values.astype(jnp.bfloat16)
    grad_query_weight = contract_rows(hidden_in.reshape(count_tok, model_width), query_low)
    grad_key_weight = contract_rows(tokens, key_low)
    grad_value_weight = contract_rows(tokens, value_low)
    input_grad = (
        grad_attended
        + times_transposed(query_low, query_weight)
        + times_transposed(key_low, key_weight)
        + times_transposed(value_low, value_weight)
    ).astype(jnp.bfloat16)
    attention_parts = (
        grad_query_weight,
        grad_query_bias,
        grad_key_weight,
        grad_value_weight,
        grad_value_bias,
        grad_out_weight,
        grad_out_bias,
        grad_first_gain,
        grad_first_shift,
    )
    summed_all = lax.psum(
        (
            grad_query_weight,
            grad_query_bias,
            grad_key_weight,
            grad_value_weight,
            grad_value_bias,
            grad_out_weight,
            grad_out_bias,
            grad_first_gain,
            grad_first_shift,
            grad_inner_weight,
            grad_inner_bias,
            grad_outer_weight,
            grad_outer_bias,
            grad_second_gain,
            grad_second_shift,
            loss_sq,
            loss_count,
        ),
        ("side", "batch"),
    )
    attention_parts = summed_all[:9]
    ffn_parts = summed_all[9:15]
    loss_sq = summed_all[15]
    loss_count = summed_all[16]
    loss = loss_sq / jnp.maximum(loss_count, 1.0)
    rows_out = final_low.reshape(1, 1, count_tok, model_width)
    input_grad = input_grad.reshape(1, 1, count_tok, model_width)
    return (
        loss,
        rows_out,
        input_grad,
        attention_parts[0],
        attention_parts[1],
        attention_parts[2],
        attention_parts[3],
        attention_parts[4],
        attention_parts[5],
        attention_parts[6],
        attention_parts[7],
        attention_parts[8],
        ffn_parts[0],
        ffn_parts[1],
        ffn_parts[2],
        ffn_parts[3],
        ffn_parts[4],
        ffn_parts[5],
    )


def solution(mesh):
    in_specs = (
        P("side", "batch", None, None),
        P("side", "batch", None),
        P("batch", None),
        P("side", "batch", None),
        P("batch"),
        P(),
        P("batch", None),
        P(),
        P(),
        P(),
        P(),
        P(),
        P(),
        P(),
        P(),
        P(),
        P(),
        P(),
        P(),
        P(),
        P(),
        P(),
    )
    out_specs = (
        P(),
        P("side", "batch", None, None),
        P("side", "batch", None, None),
        P(),
        P(),
        P(),
        P(),
        P(),
        P(),
        P(),
        P(),
        P(),
        P(),
        P(),
        P(),
        P(),
        P(),
        P(),
    )
    return jax.shard_map(body, mesh=mesh, in_specs=in_specs, out_specs=out_specs, check_vma=False)
```

profile of v0, /device:TPU:0, one launch (start us, length us, event | category | flops | bytes accessed | tf_op | source)
XLA Modules:
  0.0 664.5 jit_solution(5748049418920462220)
XLA Ops:
  16.4 3.2 fusion.79
  19.7 3.5 fusion.1
  25.4 3.8 fusion.35
  29.2 3.2 fusion.80
  32.4 3.5 fusion
  38.2 4.0 fusion.34
  44.5 23.8 %multiply_convert_fusion.2 = (bf16[1024,2048]{1,0:T(8,128)(2,1)S(1)}, f32[1024,2048]{1,0:T(8,128)}, f32[1024,2048]{1,0:T(8,128)}) fusion(f32[2048]{0:T(1024)S(1)} %copy-done.59, bf16[512,2048]{1,0:T(8,128)(2,1)S(1)} %copy-done, f32[1024,512]{0,1:T(8,128)S(1)} %get-tuple-element.126, f32[512]{0:T(512)S(1)} %copy-done.63, f32[512]{0:T(512)S(1)} %copy-done.53, ...), kind=kOutput, calls=%fused_computation.27 | convolution fusion | flops 2288517120 | bytes 25186304 | tf_op jit(solution)/shard_map/dot_general | solution.py:121
  68.4 2.7 fusion.82
  78.1 71.2 %all-gather.1 = bf16[32,5,512]{2,1,0:T(8,128)(2,1)S(1)} all-gather(bf16[1,5,512]{2,1,0:T(8,128)(2,1)S(1)} %bitcast.146), channel_id=2, replica_groups=mesh['side'=4,'batch'=8] {'side','batch'}, dimensions={0}, use_global_device_ids=true | all-gather | bytes 168960 | tf_op jit(solution)/shard_map/all_gather | solution.py:132
  155.1 2.9 copy.74
  158.1 115.9 %all-reduce.7.cloned.1.call-done = f32[160,512]{1,0:T(8,128)} async-done(((f32[160,512]{1,0:T(8,128)}), f32[160,512]{1,0:T(8,128)}) %all-reduce.7.cloned.1.call-update) | async-done | bytes 327696
  276.2 3.0 copy.75
  279.3 3.9 multiply_reduce_fusion.2
  285.4 4.5 fusion.52
  289.9 9.7 %fusion.83 = (f32[2048]{0:T(1024)}, bf16[1024,2048]{1,0:T(8,128)(2,1)S(1)}) fusion(f32[1024,2048]{1,0:T(8,128)} %get-tuple-element.108, bf16[2048,512]{1,0:T(8,128)(2,1)S(1)} %copy-done.58, f32[1024,512]{0,1:T(8,128)S(1)} %get-tuple-element.102, f32[1024,2048]{1,0:T(8,128)} %get-tuple-element.127, f32[2048]{0:T(1024)S(1)} %copy-done.59), kind=kOutput, calls=%fused_computation.157 | convolution fusion | flops 2181560320 | bytes 25182208 | tf_op jit(solution)/shard_map/dot_general | solution.py:36
  299.6 3.7 multiply_reduce_fusion.3
  303.3 4.5 fusion.18
  313.1 9.9 %multiply_reduce_fusion.1 = (f32[8,512]{1,0:T(8,128)}, f32[8,512,1024]{2,1,0:T(8,128)}) fusion(f32[8,512,1024]{2,1,0:T(8,128)S(1)} %bitcast.120, f32[8,512]{1,0:T(8,128)S(1)} %log_add_fusion.1, bf16[512,8,64]{0,2,1:T(8,128)(2,1)S(1)} %bitcast.131, bf16[1024,8,64]{0,2,1:T(8,128)(2,1)} %bitcast.137), kind=kOutput, calls=%fused_computation.8 | convolution fusion | flops 549449728 | bytes 35160064 | tf_op jit(solution)/shard_map/qhd,khd->hqk/dot_general | solution.py:209
  323.0 15.9 %multiply_convert_fusion.1 = bf16[8,512,1024]{2,1,0:T(8,128)(2,1)} fusion(f32[8,512,1024]{2,1,0:T(8,128)} %get-tuple-element.133, f32[8,512,1024]{2,1,0:T(8,128)} %copy-done.2, f32[8,512]{1,0:T(8,128)} %get-tuple-element.132, f32[8,512]{1,0:T(8,128)S(1)} %log_add_fusion.1), kind=kLoop, calls=%fused_computation.7 | loop fusion | flops 16777216 | bytes 41975808 | tf_op jit(solution)/shard_map/convert_element_type | solution.py:213
  338.9 8.2 %fusion.74 = (bf16[512,8,64]{0,2,1:T(8,128)(2,1)}, f32[8,64]{1,0:T(8,128)}) fusion(bf16[1024,8,64]{0,2,1:T(8,128)(2,1)S(1)} %bitcast.124, bf16[8,512,1024]{2,1,0:T(8,128)(2,1)} %multiply_convert_fusion.1), kind=kOutput, calls=%fused_computation.148 | convolution fusion | flops 537656832 | bytes 9963520 | tf_op jit(solution)/shard_map/hqk,khd->qhd/dot_general | solution.py:215
  347.2 6.3 fusion.84
  353.6 4.0 fusion.5
  357.6 9.9 %multiply_reduce_fusion = (f32[8,512]{1,0:T(8,128)}, f32[8,512,1024]{2,1,0:T(8,128)}) fusion(f32[8,512,1024]{2,1,0:T(8,128)S(1)} %bitcast.118, f32[8,512]{1,0:T(8,128)} %log_add_fusion, bf16[512,8,64]{0,2,1:T(8,128)(2,1)} %bitcast.133, bf16[1024,8,64]{0,2,1:T(8,128)(2,1)} %bitcast.138), kind=kOutput, calls=%fused_computation.5 | convolution fusion | flops 549449728 | bytes 35160064 | tf_op jit(solution)/shard_map/qhd,khd->hqk/dot_general | solution.py:209
  367.5 8.8 %bitcast_reduce_fusion = (f32[8,64]{1,0:T(8,128)}, bf16[8,64,1024]{2,1,0:T(8,128)(2,1)S(1)}) fusion(f32[8,64,1024]{2,1,0:T(8,128)} %fusion.5, bf16[512,8,64]{0,2,1:T(8,128)(2,1)S(1)} %bitcast.132, f32[8,512,1024]{2,1,0:T(8,128)} %copy-done.2, f32[8,512]{1,0:T(8,128)S(1)} %log_add_fusion.1), kind=kOutput, calls=%fused_computation.43 | convolution fusion | flops 546831872 | bytes 20465664 | tf_op jit(solution)/shard_map/hqk,qhd->khd/dot_general | solution.py:225
  378.1 10.5 %multiply_convert_fusion = bf16[8,512,1024]{2,1,0:T(8,128)(2,1)} fusion(f32[8,512,1024]{2,1,0:T(8,128)} %get-tuple-element.135, f32[8,512,1024]{2,1,0:T(8,128)S(1)} %bitcast.118, f32[8,512]{1,0:T(8,128)S(1)} %copy-done.38, f32[8,512]{1,0:T(8,128)S(1)} %copy-done.37), kind=kLoop, calls=%fused_computation.4 | loop fusion | flops 16777216 | bytes 41975808 | tf_op jit(solution)/shard_map/convert_element_type | solution.py:213
  388.6 6.6 fusion.75
  395.3 3.4 multiply_convert_fusion.3
  402.8 2.9 fusion.134
  408.2 43.7 %all-reduce.2 = (f32[]{:T(128)}, f32[]{:T(128)}, f32[512]{0:T(512)}, f32[512]{0:T(512)}, f32[512]{0:T(512)}, /*index=5*/f32[512]{0:T(512)}, f32[512]{0:T(512)}, ...) all-reduce(f32[]{:T(128)} %get-tuple-element.81, ...), channel_id=1, replica_groups=mesh['side'=4,'batch'=8] {'side','batch'}, use_global_device_ids=true, to_apply=%region_11.12 | all-reduce | flops 6146 | bytes 49168 | tf_op jit(solution)/shard_map/psum | solution.py:256
  459.4 181.1 %all-reduce.9.cloned.1.call-done = (f32[512,512]{0,1:T(8,128)}, f32[512,512]{0,1:T(8,128)}, f32[512,512]{0,1:T(8,128)}, f32[512,512]{1,0:T(8,128)}, f32[512,2048]{1,0:T(8,128)}, /*index=5*/f32[2048,512]{1,0:T(8,128)}) async-done(((f32[512,512]{0,1:T(8,128)}, f32[512,512]{0,1:T(8,128)}, f32[512,512]{0,1:T(8,128)}, f32[512,512]{1,0:T(8,128)}, f32[512,2048]{1,0:T(8,128)}, /*index=5*/f32[2048,512]{1,0:T(8,128)}), ...) | async-done | bytes 12582928 | tf_op jit(solution)/shard_map/psum | solution.py:256
  640.5 2.6 copy.82
  649.2 4.8 copy.98
  (213 shorter events, 60.6 us)
Async XLA Ops:
  7.2 37.3 %copy-start = (bf16[512,2048]{1,0:T(8,128)(2,1)S(1)}, bf16[512,2048]{1,0:T(8,128)(2,1)}, u32[]{:S(2)}) copy-start(bf16[512,2048]{1,0:T(8,128)(2,1)} %param.38) | copy-start | bytes 6291460
  7.2 6.9 %copy-start.25 = (bf16[1,1,1024,512]{3,2,1,0:T(8,128)(2,1)S(1)}, bf16[1,1,1024,512]{3,2,1,0:T(8,128)(2,1)}, u32[]{:S(2)}) copy-start(bf16[1,1,1024,512]{3,2,1,0:T(8,128)(2,1)} %param.22) | copy-start | bytes 3145732
  7.2 266.8 %all-reduce.7.cloned.1.call-start = ((), (), s32[]{:S(2)}) async-start(), calls=%async_computation | async-start | bytes 655360
  14.2 15.0 %copy-start.14 = (bf16[512,512]{0,1:T(8,128)(2,1)}, bf16[512,512]{0,1:T(8,128)(2,1)S(1)}, u32[]{:S(2)}) copy-start(bf16[512,512]{0,1:T(8,128)(2,1)S(1)} %get-tuple-element.115) | copy-start | bytes 1572868
  15.0 14.3 %copy-start.8 = (bf16[1024,512]{0,1:T(8,128)(2,1)}, bf16[1024,512]{0,1:T(8,128)(2,1)S(1)}, u32[]{:S(2)}) copy-start(bf16[1024,512]{0,1:T(8,128)(2,1)S(1)} %convolution_convert_fusion.1) | copy-start | bytes 3145732
  15.7 20.2 %copy-start.17 = (bf16[1024,512]{0,1:T(8,128)(2,1)}, bf16[1024,512]{0,1:T(8,128)(2,1)S(1)}, u32[]{:S(2)}) copy-start(bf16[1024,512]{0,1:T(8,128)(2,1)S(1)} %add_convert_fusion.3) | copy-start | bytes 3145732
  19.7 5.7 copy-start.1
  32.4 5.7 copy-start.2
  44.1 24.2 %copy-start.10 = (f32[1024,512]{0,1:T(8,128)}, f32[1024,512]{0,1:T(8,128)S(1)}, u32[]{:S(2)}) copy-start(f32[1024,512]{0,1:T(8,128)S(1)} %get-tuple-element.126) | copy-start | bytes 6291460
  44.5 23.9 %copy-start.57 = (bf16[2048,512]{1,0:T(8,128)(2,1)S(1)}, bf16[2048,512]{1,0:T(8,128)(2,1)}, u32[]{:S(2)}) copy-start(bf16[2048,512]{1,0:T(8,128)(2,1)} %param.40) | copy-start | bytes 6291460
  44.5 23.9 %copy-start.62 = (f32[512]{0:T(512)S(1)}, f32[512]{0:T(512)}, u32[]{:S(2)}) copy-start(f32[512]{0:T(512)} %param.41) | copy-start | bytes 6148
  71.1 78.2 %copy-start.52 = (s32[32]{0:T(128)S(1)}, s32[32]{0:T(128)}, u32[]{:S(2)}) copy-start(s32[32]{0:T(128)} %param.26) | copy-start | bytes 388
  71.2 78.2 %copy-start.56 = (s32[120]{0:T(128)S(1)}, s32[120]{0:T(128)}, u32[]{:S(2)}) copy-start(s32[120]{0:T(128)} %param.27) | copy-start | bytes 1444
  71.2 79.1 %copy-start.44 = (f32[32,120]{1,0:T(8,128)S(1)}, f32[32,120]{1,0:T(8,128)}, u32[]{:S(2)}) copy-start(f32[32,120]{1,0:T(8,128)} %param.28) | copy-start | bytes 46084
  152.1 488.4 %all-reduce.9.cloned.1.call-start = ((), (), s32[]{:S(2)}) async-start(), calls=%async_computation.1 | async-start | bytes 25165824 | tf_op jit(solution)/shard_map/psum | solution.py:256
  289.9 9.7 %copy-start.11 = (f32[1024,512]{0,1:T(8,128)S(1)}, f32[1024,512]{0,1:T(8,128)}, u32[]{:S(2)}) copy-start(f32[1024,512]{0,1:T(8,128)} %copy-done.10) | copy-start | bytes 6291460
  303.3 9.3 %slice-start.4 = ((s8[16777216]{0:T(1024)(128)(4,1)}), s8[4194304]{0:T(1024)(128)(4,1)S(1)}, s32[]{:S(2)}) async-start(s8[16777216]{0:T(1024)(128)(4,1)} %bitcast.119), calls=%async_computation.6 | async-start | bytes 8388608
  303.3 9.3 %slice-start.5 = ((s8[16777216]{0:T(1024)(128)(4,1)}), s8[4194304]{0:T(1024)(128)(4,1)S(1)}, s32[]{:S(2)}) async-start(s8[16777216]{0:T(1024)(128)(4,1)} %bitcast.119), calls=%async_computation.7 | async-start | bytes 8388608
  322.9 16.0 %copy-start.9 = (bf16[1024,512]{0,1:T(8,128)(2,1)S(1)}, bf16[1024,512]{0,1:T(8,128)(2,1)}, u32[]{:S(2)}) copy-start(bf16[1024,512]{0,1:T(8,128)(2,1)} %copy-done.8) | copy-start | bytes 3145732
  322.9 30.6 %slice-start = ((s8[16777216]{0:T(1024)(128)(4,1)}), s8[4194304]{0:T(1024)(128)(4,1)S(1)}, s32[]{:S(2)}) async-start(s8[16777216]{0:T(1024)(128)(4,1)} %bitcast.117), calls=%async_computation.2 | async-start | bytes 8388608
  322.9 30.6 %slice-start.1 = ((s8[16777216]{0:T(1024)(128)(4,1)}), s8[4194304]{0:T(1024)(128)(4,1)S(1)}, s32[]{:S(2)}) async-start(s8[16777216]{0:T(1024)(128)(4,1)} %bitcast.117), calls=%async_computation.3 | async-start | bytes 8388608
  323.0 30.6 %slice-start.2 = ((s8[16777216]{0:T(1024)(128)(4,1)}), s8[4194304]{0:T(1024)(128)(4,1)S(1)}, s32[]{:S(2)}) async-start(s8[16777216]{0:T(1024)(128)(4,1)} %bitcast.117), calls=%async_computation.4 | async-start | bytes 8388608
  338.9 8.2 %copy-start.15 = (bf16[512,512]{0,1:T(8,128)(2,1)S(1)}, bf16[512,512]{0,1:T(8,128)(2,1)}, u32[]{:S(2)}) copy-start(bf16[512,512]{0,1:T(8,128)(2,1)} %copy-done.14) | copy-start | bytes 1572868
  338.9 14.6 %slice-start.3 = ((s8[16777216]{0:T(1024)(128)(4,1)}), s8[4194304]{0:T(1024)(128)(4,1)S(1)}, s32[]{:S(2)}) async-start(s8[16777216]{0:T(1024)(128)(4,1)} %bitcast.117), calls=%async_computation.5 | async-start | bytes 8388608
  347.2 6.4 copy-start.16
  347.2 6.4 copy-start.36
  367.5 8.8 %copy-start.26 = (bf16[1,1,1024,512]{3,2,1,0:T(8,128)(2,1)S(1)}, bf16[1,1,1024,512]{3,2,1,0:T(8,128)(2,1)}, u32[]{:S(2)}) copy-start(bf16[1,1,1024,512]{3,2,1,0:T(8,128)(2,1)} %param.22) | copy-start | bytes 3145732
  367.5 10.6 %copy-start.37 = (f32[8,512]{1,0:T(8,128)S(1)}, f32[8,512]{1,0:T(8,128)}, u32[]{:S(2)}) copy-start(f32[8,512]{1,0:T(8,128)} %log_add_fusion) | copy-start | bytes 49156
  367.5 10.6 %copy-start.38 = (f32[8,512]{1,0:T(8,128)S(1)}, f32[8,512]{1,0:T(8,128)}, u32[]{:S(2)}) copy-start(f32[8,512]{1,0:T(8,128)} %get-tuple-element.134) | copy-start | bytes 49156
  388.6 6.6 copy-start.3
  388.6 6.6 copy-start.13
  640.5 7.7 %copy-start.28 = (f32[512,512]{1,0:T(8,128)S(1)}, f32[512,512]{1,0:T(8,128)}, u32[]{:S(2)}) copy-start(f32[512,512]{1,0:T(8,128)} %get-tuple-element.156) | copy-start | bytes 3145732
  (44 other events, 160.4 us)
Sparse Core Ops, SparseCore 0:
  152.2 121.7 all-reduce.6
  402.2 238.2 all-reduce.8
where the time goes:
time: 674 us; the launch traced here: 664 us
  waiting for transfers between devices  297 us (44%)
  matrix products  138 us (20%)
  blocking collectives  115 us (17%)
  other arithmetic  53.7 us (8%)
  local copies, waits for them, and re-layouts  43.2 us (6%)
  between operations  17.9 us (3%)
    psum x1, waiting for transfers between devices, body(): lax.psum((grad_query_weight, grad_query_bias, grad_key_weight, grad_value...  181 us
    unnamed x3, waiting for transfers between devices  116 us
    all_gather x1, blocking collectives, body(): lax.all_gather(passage_vectors, ('side', 'batch'), axis=0, tiled=True)  71.2 us
    psum x1, blocking collectives, body(): lax.psum((grad_query_weight, grad_query_bias, grad_key_weight, grad_value...  43.7 us
    unnamed x157, local copies, waits for them, and re-layouts  30.1 us
    convert_element_type x2, other arithmetic, body(): grad_scores = (probs * (grad_probs - row_dot)).astype(jnp.bfloat16)  26.4 us
    dot_general x1, matrix products, body(): jnp.dot(first_low, inner_weight, preferred_element_type=jnp.float32)  23.8 us
    dot_general x2, matrix products, body(): jnp.einsum('qhd,khd->hqk', upstream, values3, preferred_element_type=jnp....  19.8 us
  transfers between devices with their start and end apart: 2, of which 2 were waited for; matrix products, arithmetic and copies ran while one was open for 3% of the time, Pallas kernels for 0%

commit v1 on v0

--- a/solution.py
+++ b/solution.py
@@ -129,7 +129,15 @@
     final_low = final.astype(jnp.bfloat16)
     query_vectors = final_low[query_idx]
     passage_vectors = final_low[passage_idx]
-    gathered = lax.all_gather(passage_vectors, ("side", "batch"), axis=0, tiled=True)
+    ways, here = (lax.axis_size(("side", "batch")), lax.axis_index(("side", "batch")))
+    grown, reach = (passage_vectors, 1)
+    while reach < ways:
+        theirs = lax.ppermute(grown, ("side", "batch"), [(d, d ^ reach) for d in range(ways)])
+        mine_first = jnp.concatenate([grown, theirs], axis=0)
+        theirs_first = jnp.concatenate([theirs, grown], axis=0)
+        grown = jnp.where(here & reach == 0, mine_first, theirs_first)
+        reach = 2 * reach
+    gathered = grown
     pass_count = teacher.shape[1]
     front = gathered.shape[0] - pass_count
     passages_all = gathered[front:]

time: 674 us -> 626 us (0.929)
  blocking collectives: 115 us -> 43.8 us
  waiting for transfers between devices: 297 us -> 311 us
  starting transfers between devices: 0.08 us -> 10.3 us
    all_gather x1 -> x0, blocking collectives: 71.2 us -> none  [body(): lax.all_gather(passage_vectors, ('side', 'batch'), axis=0, tiled=True)]
    ppermute x0 -> x5, starting transfers between devices: none -> 10.3 us  [body(): lax.ppermute(grown, ('side', 'batch'), [(d, d ^ reach) for d in range(way...]
    ppermute x0 -> x5, waiting for transfers between devices: none -> 7.41 us  [body(): lax.ppermute(grown, ('side', 'batch'), [(d, d ^ reach) for d in range(way...]
    unnamed x157 -> x159, local copies, waits for them, and re-layouts: 30.1 us -> 30.2 us
  transfers between devices with their start and end apart: 2 -> 7, of which waited for: 2 -> 6; matrix products, arithmetic and copies ran while one was open for 3% -> 3% of each run, Pallas kernels for 0% -> 0%
where the time goes in v1:
time: 626 us; the launch traced here: 617 us
  waiting for transfers between devices  311 us (50%)
  matrix products  138 us (22%)
  other arithmetic  53.2 us (8%)
  blocking collectives  43.8 us (7%)
  local copies, waits for them, and re-layouts  43.2 us (7%)
  between operations  17.9 us (3%)
  starting transfers between devices  10.3 us (2%)
    psum x1, waiting for transfers between devices, body(): lax.psum((grad_query_weight, grad_query_bias, grad_key_weight, grad_value...  181 us
    unnamed x3, waiting for transfers between devices  122 us
    psum x1, blocking collectives, body(): lax.psum((grad_query_weight, grad_query_bias, grad_key_weight, grad_value...  43.8 us
    unnamed x159, local copies, waits for them, and re-layouts  30.2 us
    convert_element_type x2, other arithmetic, body(): grad_scores = (probs * (grad_probs - row_dot)).astype(jnp.bfloat16)  26.4 us
    dot_general x1, matrix products, body(): jnp.dot(first_low, inner_weight, preferred_element_type=jnp.float32)  23.8 us
    dot_general x2, matrix products, body(): jnp.einsum('qhd,khd->hqk', upstream, values3, preferred_element_type=jnp....  19.8 us
    dot_general x7, matrix products, times_transposed(): lax.dot_general(left, right, (((1,), (1,)), ((), ())), preferred_element_...  18.1 us
  transfers between devices with their start and end apart: 7, of which 6 were waited for; matrix products, arithmetic and copies ran while one was open for 3% of the time, Pallas kernels for 0%

profile of v1, /device:TPU:0, one launch (start us, length us, event | category | flops | bytes accessed | tf_op | source)
XLA Modules:
  0.0 616.8 jit_solution(10356182086103635557)
XLA Ops:
  15.7 3.2 fusion.84
  19.0 3.5 fusion.1
  24.7 3.8 fusion.35
  28.5 3.2 fusion.85
  31.8 3.5 fusion
  37.5 4.0 fusion.34
  43.9 23.8 %multiply_convert_fusion.2 = (bf16[1024,2048]{1,0:T(8,128)(2,1)S(1)}, f32[1024,2048]{1,0:T(8,128)}, f32[1024,2048]{1,0:T(8,128)}) fusion(f32[2048]{0:T(1024)S(1)} %copy-done.59, bf16[512,2048]{1,0:T(8,128)(2,1)S(1)} %copy-done, f32[1024,512]{0,1:T(8,128)S(1)} %get-tuple-element.126, f32[512]{0:T(512)S(1)} %copy-done.63, f32[512]{0:T(512)S(1)} %copy-done.52, ...), kind=kOutput, calls=%fused_computation.27 | convolution fusion | flops 2288517120 | bytes 25186304 | tf_op jit(solution)/shard_map/dot_general | solution.py:121
  75.5 3.0 collective-permute-start
  84.0 3.1 collective-permute-start.2
  93.2 2.9 collective-permute-done.4
  101.1 3.0 copy.74
  104.1 122.0 %all-reduce.7.cloned.1.call-done = f32[160,512]{1,0:T(8,128)} async-done(((f32[160,512]{1,0:T(8,128)}), f32[160,512]{1,0:T(8,128)}) %all-reduce.7.cloned.1.call-update) | async-done | bytes 327696
  228.3 3.0 copy.75
  231.4 3.9 multiply_reduce_fusion.2
  237.5 4.5 fusion.52
  242.0 9.7 %fusion.88 = (f32[2048]{0:T(1024)}, bf16[1024,2048]{1,0:T(8,128)(2,1)S(1)}) fusion(f32[1024,2048]{1,0:T(8,128)} %get-tuple-element.108, bf16[2048,512]{1,0:T(8,128)(2,1)S(1)} %copy-done.58, f32[1024,512]{0,1:T(8,128)S(1)} %get-tuple-element.102, f32[1024,2048]{1,0:T(8,128)} %get-tuple-element.127, f32[2048]{0:T(1024)S(1)} %copy-done.59), kind=kOutput, calls=%fused_computation.166 | convolution fusion | flops 2181560320 | bytes 25182208 | tf_op jit(solution)/shard_map/dot_general | solution.py:36
  251.7 3.7 multiply_reduce_fusion.3
  255.4 4.5 fusion.18
  265.2 9.9 %multiply_reduce_fusion.1 = (f32[8,512]{1,0:T(8,128)}, f32[8,512,1024]{2,1,0:T(8,128)}) fusion(f32[8,512,1024]{2,1,0:T(8,128)S(1)} %bitcast.117, f32[8,512]{1,0:T(8,128)S(1)} %log_add_fusion.1, bf16[512,8,64]{0,2,1:T(8,128)(2,1)S(1)} %bitcast.128, bf16[1024,8,64]{0,2,1:T(8,128)(2,1)} %bitcast.134), kind=kOutput, calls=%fused_computation.8 | convolution fusion | flops 549449728 | bytes 35160064 | tf_op jit(solution)/shard_map/qhd,khd->hqk/dot_general | solution.py:217
  275.1 15.9 %multiply_convert_fusion.1 = bf16[8,512,1024]{2,1,0:T(8,128)(2,1)} fusion(f32[8,512,1024]{2,1,0:T(8,128)} %get-tuple-element.133, f32[8,512,1024]{2,1,0:T(8,128)} %copy-done.2, f32[8,512]{1,0:T(8,128)} %get-tuple-element.132, f32[8,512]{1,0:T(8,128)S(1)} %log_add_fusion.1), kind=kLoop, calls=%fused_computation.7 | loop fusion | flops 16777216 | bytes 41975808 | tf_op jit(solution)/shard_map/convert_element_type | solution.py:221
  291.1 8.2 %fusion.79 = (bf16[512,8,64]{0,2,1:T(8,128)(2,1)}, f32[8,64]{1,0:T(8,128)}) fusion(bf16[1024,8,64]{0,2,1:T(8,128)(2,1)S(1)} %bitcast.121, bf16[8,512,1024]{2,1,0:T(8,128)(2,1)} %multiply_convert_fusion.1), kind=kOutput, calls=%fused_computation.157 | convolution fusion | flops 537656832 | bytes 9963520 | tf_op jit(solution)/shard_map/hqk,khd->qhd/dot_general | solution.py:223
  299.3 6.3 %fusion.89 = f32[8,64,1024]{2,1,0:T(8,128)} fusion(bf16[512,8,64]{0,2,1:T(8,128)(2,1)S(1)} %bitcast.127, bf16[8,512,1024]{2,1,0:T(8,128)(2,1)} %multiply_convert_fusion.1), kind=kOutput, calls=%fused_computation.167 | convolution fusion | flops 536870912 | bytes 11010048 | tf_op jit(solution)/shard_map/hqk,qhd->khd/dot_general | solution.py:228
  305.7 4.0 fusion.5
  309.7 10.0 %multiply_reduce_fusion = (f32[8,512]{1,0:T(8,128)}, f32[8,512,1024]{2,1,0:T(8,128)}) fusion(f32[8,512,1024]{2,1,0:T(8,128)S(1)} %bitcast.115, f32[8,512]{1,0:T(8,128)} %log_add_fusion, bf16[512,8,64]{0,2,1:T(8,128)(2,1)} %bitcast.130, bf16[1024,8,64]{0,2,1:T(8,128)(2,1)} %bitcast.135), kind=kOutput, calls=%fused_computation.5 | convolution fusion | flops 549449728 | bytes 35160064 | tf_op jit(solution)/shard_map/qhd,khd->hqk/dot_general | solution.py:217
  319.7 8.8 %bitcast_reduce_fusion = (f32[8,64]{1,0:T(8,128)}, bf16[8,64,1024]{2,1,0:T(8,128)(2,1)S(1)}) fusion(f32[8,64,1024]{2,1,0:T(8,128)} %fusion.5, bf16[512,8,64]{0,2,1:T(8,128)(2,1)S(1)} %bitcast.129, f32[8,512,1024]{2,1,0:T(8,128)} %copy-done.2, f32[8,512]{1,0:T(8,128)S(1)} %log_add_fusion.1), kind=kOutput, calls=%fused_computation.43 | convolution fusion | flops 546831872 | bytes 20465664 | tf_op jit(solution)/shard_map/hqk,qhd->khd/dot_general | solution.py:233
  330.3 10.5 %multiply_convert_fusion = bf16[8,512,1024]{2,1,0:T(8,128)(2,1)} fusion(f32[8,512,1024]{2,1,0:T(8,128)} %get-tuple-element.135, f32[8,512,1024]{2,1,0:T(8,128)S(1)} %bitcast.115, f32[8,512]{1,0:T(8,128)S(1)} %copy-done.38, f32[8,512]{1,0:T(8,128)S(1)} %copy-done.37), kind=kLoop, calls=%fused_computation.4 | loop fusion | flops 16777216 | bytes 41975808 | tf_op jit(solution)/shard_map/convert_element_type | solution.py:221
  340.8 6.6 %fusion.80 = (bf16[512,8,64]{0,2,1:T(8,128)(2,1)S(1)}, f32[8,64]{1,0:T(8,128)S(1)}) fusion(bf16[1024,8,64]{0,2,1:T(8,128)(2,1)} %bitcast.120, bf16[8,512,1024]{2,1,0:T(8,128)(2,1)} %multiply_convert_fusion), kind=kOutput, calls=%fused_computation.158 | convolution fusion | flops 537656832 | bytes 9963520 | tf_op jit(solution)/shard_map/hqk,khd->qhd/dot_general | solution.py:223
  347.5 3.4 multiply_convert_fusion.3
  355.0 2.9 fusion.137
  360.4 43.8 %all-reduce.2 = (f32[]{:T(128)}, f32[]{:T(128)}, f32[512]{0:T(512)}, f32[512]{0:T(512)}, f32[512]{0:T(512)}, /*index=5*/f32[512]{0:T(512)}, f32[512]{0:T(512)}, ...) all-reduce(f32[]{:T(128)} %get-tuple-element.81, ...), channel_id=1, replica_groups=mesh['side'=4,'batch'=8] {'side','batch'}, use_global_device_ids=true, to_apply=%region_11.12 | all-reduce | flops 6146 | bytes 49168 | tf_op jit(solution)/shard_map/psum | solution.py:264
  411.7 181.1 %all-reduce.9.cloned.1.call-done = (f32[512,512]{0,1:T(8,128)}, f32[512,512]{0,1:T(8,128)}, f32[512,512]{0,1:T(8,128)}, f32[512,512]{1,0:T(8,128)}, f32[512,2048]{1,0:T(8,128)}, /*index=5*/f32[2048,512]{1,0:T(8,128)}) async-done(((f32[512,512]{0,1:T(8,128)}, f32[512,512]{0,1:T(8,128)}, f32[512,512]{0,1:T(8,128)}, f32[512,512]{1,0:T(8,128)}, f32[512,2048]{1,0:T(8,128)}, /*index=5*/f32[2048,512]{1,0:T(8,128)}), ...) | async-done | bytes 12582928 | tf_op jit(solution)/shard_map/psum | solution.py:264
  601.4 4.8 copy.98
  (226 shorter events, 74.1 us)
Async XLA Ops:
  7.2 36.6 %copy-start = (bf16[512,2048]{1,0:T(8,128)(2,1)S(1)}, bf16[512,2048]{1,0:T(8,128)(2,1)}, u32[]{:S(2)}) copy-start(bf16[512,2048]{1,0:T(8,128)(2,1)} %param.38) | copy-start | bytes 6291460
  7.2 218.9 %all-reduce.7.cloned.1.call-start = ((), (), s32[]{:S(2)}) async-start(), calls=%async_computation | async-start | bytes 655360
  13.5 15.0 %copy-start.14 = (bf16[512,512]{0,1:T(8,128)(2,1)}, bf16[512,512]{0,1:T(8,128)(2,1)S(1)}, u32[]{:S(2)}) copy-start(bf16[512,512]{0,1:T(8,128)(2,1)S(1)} %get-tuple-element.115) | copy-start | bytes 1572868
  14.3 14.3 %copy-start.8 = (bf16[1024,512]{0,1:T(8,128)(2,1)}, bf16[1024,512]{0,1:T(8,128)(2,1)S(1)}, u32[]{:S(2)}) copy-start(bf16[1024,512]{0,1:T(8,128)(2,1)S(1)} %convolution_convert_fusion.1) | copy-start | bytes 3145732
  15.0 20.3 %copy-start.17 = (bf16[1024,512]{0,1:T(8,128)(2,1)}, bf16[1024,512]{0,1:T(8,128)(2,1)S(1)}, u32[]{:S(2)}) copy-start(bf16[1024,512]{0,1:T(8,128)(2,1)S(1)} %add_convert_fusion.3) | copy-start | bytes 3145732
  43.5 24.3 %copy-start.10 = (f32[1024,512]{0,1:T(8,128)}, f32[1024,512]{0,1:T(8,128)S(1)}, u32[]{:S(2)}) copy-start(f32[1024,512]{0,1:T(8,128)S(1)} %get-tuple-element.126) | copy-start | bytes 6291460
  43.9 23.9 %copy-start.57 = (bf16[2048,512]{1,0:T(8,128)(2,1)S(1)}, bf16[2048,512]{1,0:T(8,128)(2,1)}, u32[]{:S(2)}) copy-start(bf16[2048,512]{1,0:T(8,128)(2,1)} %param.40) | copy-start | bytes 6291460
  43.9 23.9 %copy-start.62 = (f32[512]{0:T(512)S(1)}, f32[512]{0:T(512)}, u32[]{:S(2)}) copy-start(f32[512]{0:T(512)} %param.41) | copy-start | bytes 6148
  70.5 16.6 %copy-start.64 = (s32[1,32]{1,0:T(1,128)S(1)}, s32[1,32]{1,0:T(1,128)}, u32[]{:S(2)}) copy-start(s32[1,32]{1,0:T(1,128)} %param.24) | copy-start | bytes 388
  70.5 22.5 %copy-start.53 = (s32[32]{0:T(128)S(1)}, s32[32]{0:T(128)}, u32[]{:S(2)}) copy-start(s32[32]{0:T(128)} %param.26) | copy-start | bytes 388
  70.5 22.5 %copy-start.56 = (s32[120]{0:T(128)S(1)}, s32[120]{0:T(128)}, u32[]{:S(2)}) copy-start(s32[120]{0:T(128)} %param.27) | copy-start | bytes 1444
  70.5 26.3 %copy-start.44 = (f32[32,120]{1,0:T(8,128)S(1)}, f32[32,120]{1,0:T(8,128)}, u32[]{:S(2)}) copy-start(f32[32,120]{1,0:T(8,128)} %param.28) | copy-start | bytes 46084
  75.5 4.6 collective-permute-start
  80.1 3.9 collective-permute-start.1
  84.0 4.9 collective-permute-start.2
  89.0 2.1 collective-permute-start.3
  91.1 5.0 collective-permute-start.4
  98.7 494.1 %all-reduce.9.cloned.1.call-start = ((), (), s32[]{:S(2)}) async-start(), calls=%async_computation.1 | async-start | bytes 25165824 | tf_op jit(solution)/shard_map/psum | solution.py:264
  242.0 9.7 %copy-start.11 = (f32[1024,512]{0,1:T(8,128)S(1)}, f32[1024,512]{0,1:T(8,128)}, u32[]{:S(2)}) copy-start(f32[1024,512]{0,1:T(8,128)} %copy-done.10) | copy-start | bytes 6291460
  255.4 9.3 %slice-start.4 = ((s8[16777216]{0:T(1024)(128)(4,1)}), s8[4194304]{0:T(1024)(128)(4,1)S(1)}, s32[]{:S(2)}) async-start(s8[16777216]{0:T(1024)(128)(4,1)} %bitcast.116), calls=%async_computation.6 | async-start | bytes 8388608
  255.4 9.3 %slice-start.5 = ((s8[16777216]{0:T(1024)(128)(4,1)}), s8[4194304]{0:T(1024)(128)(4,1)S(1)}, s32[]{:S(2)}) async-start(s8[16777216]{0:T(1024)(128)(4,1)} %bitcast.116), calls=%async_computation.7 | async-start | bytes 8388608
  275.1 15.9 %copy-start.9 = (bf16[1024,512]{0,1:T(8,128)(2,1)S(1)}, bf16[1024,512]{0,1:T(8,128)(2,1)}, u32[]{:S(2)}) copy-start(bf16[1024,512]{0,1:T(8,128)(2,1)} %copy-done.8) | copy-start | bytes 3145732
  275.1 30.5 %slice-start = ((s8[16777216]{0:T(1024)(128)(4,1)}), s8[4194304]{0:T(1024)(128)(4,1)S(1)}, s32[]{:S(2)}) async-start(s8[16777216]{0:T(1024)(128)(4,1)} %bitcast.114), calls=%async_computation.2 | async-start | bytes 8388608
  275.1 30.5 %slice-start.1 = ((s8[16777216]{0:T(1024)(128)(4,1)}), s8[4194304]{0:T(1024)(128)(4,1)S(1)}, s32[]{:S(2)}) async-start(s8[16777216]{0:T(1024)(128)(4,1)} %bitcast.114), calls=%async_computation.3 | async-start | bytes 8388608
  275.1 30.5 %slice-start.2 = ((s8[16777216]{0:T(1024)(128)(4,1)}), s8[4194304]{0:T(1024)(128)(4,1)S(1)}, s32[]{:S(2)}) async-start(s8[16777216]{0:T(1024)(128)(4,1)} %bitcast.114), calls=%async_computation.4 | async-start | bytes 8388608
  291.0 8.3 %copy-start.15 = (bf16[512,512]{0,1:T(8,128)(2,1)S(1)}, bf16[512,512]{0,1:T(8,128)(2,1)}, u32[]{:S(2)}) copy-start(bf16[512,512]{0,1:T(8,128)(2,1)} %copy-done.14) | copy-start | bytes 1572868
  291.0 14.6 %slice-start.3 = ((s8[16777216]{0:T(1024)(128)(4,1)}), s8[4194304]{0:T(1024)(128)(4,1)S(1)}, s32[]{:S(2)}) async-start(s8[16777216]{0:T(1024)(128)(4,1)} %bitcast.114), calls=%async_computation.5 | async-start | bytes 8388608
  319.7 8.8 %copy-start.26 = (bf16[1,1,1024,512]{3,2,1,0:T(8,128)(2,1)S(1)}, bf16[1,1,1024,512]{3,2,1,0:T(8,128)(2,1)}, u32[]{:S(2)}) copy-start(bf16[1,1,1024,512]{3,2,1,0:T(8,128)(2,1)} %param.22) | copy-start | bytes 3145732
  319.7 10.6 %copy-start.37 = (f32[8,512]{1,0:T(8,128)S(1)}, f32[8,512]{1,0:T(8,128)}, u32[]{:S(2)}) copy-start(f32[8,512]{1,0:T(8,128)} %log_add_fusion) | copy-start | bytes 49156
  319.7 10.6 %copy-start.38 = (f32[8,512]{1,0:T(8,128)S(1)}, f32[8,512]{1,0:T(8,128)}, u32[]{:S(2)}) copy-start(f32[8,512]{1,0:T(8,128)} %get-tuple-element.134) | copy-start | bytes 49156
  340.8 6.6 %copy-start.3 = (bf16[8,512,1024]{2,1,0:T(8,128)(2,1)S(1)}, bf16[8,512,1024]{2,1,0:T(8,128)(2,1)}, u32[]{:S(2)}) copy-start(bf16[8,512,1024]{2,1,0:T(8,128)(2,1)} %multiply_convert_fusion) | copy-start | bytes 25165828
  592.8 7.7 %copy-start.28 = (f32[512,512]{1,0:T(8,128)S(1)}, f32[512,512]{1,0:T(8,128)}, u32[]{:S(2)}) copy-start(f32[512,512]{1,0:T(8,128)} %get-tuple-element.156) | copy-start | bytes 3145732
  (50 other events, 197.5 us)
Sparse Core Ops, SparseCore 0:
  98.8 127.2 all-reduce.6
  354.4 238.3 all-reduce.8
